TPU v7x, 512 devices: a whole 4x4x16 slice. The times are simulated.
512 devices in a mesh: gz: 128 (over z, y, core), row: 4 (over x).
Axes of the slice: x: 4, y: 4, z: 16, core: 2. Of those that a mesh axis runs over, the one named last changes fastest.
Arguments:
- tokens: bfloat16 [262144, 384], P(('gz', 'row')), may hold values from -6 to 6
- key_blocks: int32 [4096, 20], P(('gz', 'row')), may hold values from 0 to 4095, as said below
- counts: int32 [128], replicated, may hold values from 8 to 32, as said below
- norm_gain: float32 [384], replicated, may hold values from 0.1 to 1.9
- qkv_weight: bfloat16 [384, 1152], replicated, may hold values from -1 to 1
- out_weight: bfloat16 [384, 384], replicated, may hold values from -0.3125 to 0.3125
- mlp_gain: float32 [384], replicated, may hold values from 0.1 to 1.9
- up_weight: bfloat16 [384, 1536], replicated, may hold values from -0.3125 to 0.3125
- down_weight: bfloat16 [1536, 384], replicated, may hold values from -0.15625 to 0.15625
Outputs:
- block_out: bfloat16 [262144, 384], P(('gz', 'row'))
Inputs may be any that keep to these rules, and one draw needn't show every extreme that they name: `key_blocks`: entries 0 to 3 of a query block's list name live blocks of the query's own slab (repeats possible). The other 16 entries name blocks with the same row group as the query block (id % 32 // 8 equal), in any slab; over the blocks of one device each slab is named by exactly 1 such entries. `counts`: one slab is full in every draw.
All inputs are finite; a program needn't handle non-finite values.
Results may differ from a plain program's by a relative error of at most 0.01.
Values may be sent and summed in bfloat16 or wider, within the bound.
A program may use at most 128 MiB of HBM per device.

v0:
```python
import jax
import jax.numpy as jnp
from jax import lax
from jax.sharding import PartitionSpec as P

H = 12
NNEAR = 4
NFAR = 16


def rms_norm(values, gain):
    mean_sq = jnp.mean(values * values, axis=-1, keepdims=True)
    return values * lax.rsqrt(mean_sq + 1e-05) * gain


def attend(query_block, key_values, live_blocks):
    model_width = query_block.shape[1]
    head_size = model_width // H
    keys = key_values[:, :, :model_width].reshape(-1, H, head_size)
    values = key_values[:, :, model_width:].reshape(-1, H, head_size)
    heads = query_block.reshape(-1, H, head_size)
    scores = jnp.einsum("qhd,khd->hqk", heads, keys, preferred_element_type=jnp.float32) / jnp.sqrt(
        jnp.float32(head_size)
    )
    key_live = jnp.repeat(live_blocks, key_values.shape[1])
    scores = jnp.where(key_live[None, None, :], scores, jnp.float32(-1e30))
    top = jnp.max(scores, axis=-1, keepdims=True)
    weights = jnp.exp(scores - top)
    total = jnp.sum(weights, axis=-1)
    mixed = jnp.einsum(
        "hqk,khd->qhd", weights.astype(jnp.bfloat16), values, preferred_element_type=jnp.float32
    )
    mixed = mixed / jnp.transpose(total)[:, :, None]
    return mixed.reshape(-1, model_width).astype(jnp.bfloat16)


def body(
    tokens, key_blocks, counts, norm_gain, qkv_weight, out_weight, mlp_gain, up_weight, down_weight
):
    model_width = tokens.shape[1]
    own_blocks = key_blocks.shape[0]
    block_len = tokens.shape[0] // own_blocks
    slabs_n = lax.axis_size("gz")
    slab_blocks = own_blocks * lax.axis_size("row")
    inputs = tokens.astype(jnp.float32)
    normed = rms_norm(inputs, norm_gain).astype(jnp.bfloat16)
    projected = jnp.dot(normed, qkv_weight, preferred_element_type=jnp.float32).astype(jnp.bfloat16)
    queries = projected[:, :model_width].reshape(own_blocks, block_len, model_width)
    kv_own = projected[:, model_width:].reshape(own_blocks, block_len, 2 * model_width)
    slab_kv = lax.all_gather(kv_own, "row", axis=0, tiled=True)
    owner_slab = key_blocks // slab_blocks
    within = key_blocks % slab_blocks
    slab_table = jnp.arange(slabs_n, dtype=jnp.int32)
    slab_count = jnp.sum(jnp.where(owner_slab[:, :, None] == slab_table, counts, 0), axis=-1)
    live = within < slab_count
    near_rows = within[:, :NNEAR]
    far_owner = owner_slab[:, NNEAR:].reshape(-1)
    far_local = (key_blocks[:, NNEAR:] % own_blocks).reshape(-1)
    request_count = far_owner.shape[0]
    per_owner = request_count // slabs_n
    slab_hits = (far_owner[:, None] == slab_table[None, :]).astype(jnp.int32)
    slot_rank = jnp.sum((jnp.cumsum(slab_hits, axis=0) - 1) * slab_hits, axis=1)
    far_slot = far_owner * per_owner + slot_rank
    slot_hits = far_slot[:, None] == jnp.arange(request_count, dtype=jnp.int32)[None, :]
    request = jnp.sum(jnp.where(slot_hits, far_local[:, None], 0), axis=0)
    wanted = lax.all_to_all(
        request.reshape(slabs_n, per_owner), "gz", split_axis=0, concat_axis=0, tiled=True
    ).reshape(-1)
    kv_sent = kv_own[wanted].reshape(slabs_n, per_owner, block_len, 2 * model_width)
    far_kv = lax.all_to_all(kv_sent, "gz", split_axis=0, concat_axis=0, tiled=True).reshape(
        request_count, block_len, 2 * model_width
    )
    far_slots = far_slot.reshape(own_blocks, NFAR)

    def one_block(packed):
        query_block, near_row, slot_row, live_blocks = packed
        gathered = jnp.concatenate([slab_kv[near_row], far_kv[slot_row]], axis=0)
        return attend(query_block, gathered, live_blocks)

    attended = lax.map(one_block, (queries, near_rows, far_slots, live)).reshape(-1, model_width)
    residual = (inputs + jnp.dot(attended, out_weight, preferred_element_type=jnp.float32)).astype(
        jnp.bfloat16
    )
    normed_two = rms_norm(residual.astype(jnp.float32), mlp_gain).astype(jnp.bfloat16)
    hidden = jax.nn.gelu(jnp.dot(normed_two, up_weight, preferred_element_type=jnp.float32)).astype(
        jnp.bfloat16
    )
    result = residual.astype(jnp.float32) + jnp.dot(
        hidden, down_weight, preferred_element_type=jnp.float32
    )
    return result.astype(jnp.bfloat16)


def solution(mesh):
    return jax.shard_map(
        body,
        mesh=mesh,
        in_specs=(
            P(("gz", "row"), None),
            P(("gz", "row"), None),
            P(),
            P(),
            P(),
            P(),
            P(),
            P(),
            P(),
        ),
        out_specs=P(("gz", "row"), None),
        check_vma=False,
    )
```

profile of v0, /device:TPU:34, one launch (start us, length us, event | category | flops | bytes accessed | tf_op | source)
XLA Modules:
  0.0 899.9 jit_solution(1121670228715320951)
XLA Ops:
  9.8 19.2 %all-to-all-start = ((s32[128,1,1]{2,1,0:T(1,128)}), s32[128,1,1]{2,1,0:T(1,128)S(1)}, u32[]{:S(2)}, u32[]{:S(2)}) async-start(s32[128,1,1]{2,1,0:T(1,128)} %copy.50), calls=%async_computation | async-start | bytes 131072 | tf_op jit(solution)/shard_map/all_to_all | solution.py:66
  33.1 10.2 %all-to-all-done = s32[128,1,1]{2,1,0:T(1,128)S(1)} async-done(((s32[128,1,1]{2,1,0:T(1,128)}), s32[128,1,1]{2,1,0:T(1,128)S(1)}, u32[]{:S(2)}, u32[]{:S(2)}) %all-to-all-start) | async-done | bytes 544 | tf_op jit(solution)/shard_map/all_to_all | solution.py:66
  45.6 8.3 gather_fusion.2
  53.9 7.6 all-to-all-start.1
  65.7 46.3 %all-gather.2.cloned.1.call-done = bf16[32,64,768]{2,1,0:T(8,128)(2,1)} async-done(((bf16[8,64,768]{2,1,0:T(8,128)(2,1)}), bf16[32,64,768]{2,1,0:T(8,128)(2,1)}) %all-gather.2.cloned.1.call-update) | async-done | bytes 3145744 | tf_op jit(solution)/shard_map/all_gather | solution.py:50
  112.0 496.7 %all-to-all-done.1 = bf16[128,1,64,768]{3,2,1,0:T(8,128)(2,1)} async-done(((bf16[128,1,64,768]{3,2,1,0:T(8,128)(2,1)}), bf16[128,1,64,768]{3,2,1,0:T(8,128)(2,1)}, u32[]{:S(2)}, u32[]{:S(2)}) %all-to-all-start.1) | async-done | bytes 12582944 | tf_op jit(solution)/shard_map/all_to_all | solution.py:70
  608.7 278.2 %while.10 = (s32[]{:T(128)}, bf16[8,64,384]{2,1,0:T(8,128)(2,1)}, s32[8,4]{1,0:T(8,128)}, bf16[32,64,768]{2,1,0:T(8,128)(2,1)}, s32[8,16]{1,0:T(8,128)}, /*index...) while((s32[]{:T(128)}, bf16[8,64,384]{2,1,0:T(8,128)(2,1)}, ...), condition=%wide.region_8.9_spmd, body=%wide.region_5.8_spmd.sunk | while | flops 132760128 | bytes 49673220 | solution.py:80
  610.1 2.5 gather_fusion
  613.4 5.2 gather_fusion.1
  619.9 3.0 fusion.76
  622.9 2.8 copy.69
  625.7 2.4 reshape.201
  634.4 2.8 copy.67
  639.6 3.1 fusion.79
  644.9 2.5 gather_fusion
  648.1 5.2 gather_fusion.1
  654.7 3.0 fusion.76
  657.6 2.8 copy.69
  660.4 2.4 reshape.201
  669.2 2.8 copy.67
  674.4 3.1 fusion.79
  679.6 2.5 gather_fusion
  682.9 5.2 gather_fusion.1
  689.4 3.0 fusion.76
  692.4 2.8 copy.69
  695.2 2.4 reshape.201
  704.0 2.8 copy.67
  709.2 3.1 fusion.79
  714.4 2.5 gather_fusion
  717.7 5.2 gather_fusion.1
  724.2 3.0 fusion.76
  727.2 2.8 copy.69
  730.0 2.4 reshape.201
  738.8 2.8 copy.67
  743.9 3.1 fusion.79
  749.2 2.5 gather_fusion
  752.5 5.2 gather_fusion.1
  759.0 3.0 fusion.76
  762.0 2.8 copy.69
  764.8 2.4 reshape.201
  773.5 2.8 copy.67
  778.7 3.1 fusion.79
  784.0 2.5 gather_fusion
  787.2 5.2 gather_fusion.1
  793.8 3.0 fusion.76
  796.7 2.8 copy.69
  799.5 2.4 reshape.201
  808.3 2.8 copy.67
  813.5 3.1 fusion.79
  818.7 2.5 gather_fusion
  822.0 5.2 gather_fusion.1
  828.5 3.0 fusion.76
  831.5 2.8 copy.69
  834.3 2.4 reshape.201
  843.1 2.8 copy.67
  848.3 3.1 fusion.79
  853.5 2.5 gather_fusion
  856.8 5.2 gather_fusion.1
  863.3 3.0 fusion.76
  866.3 2.8 copy.69
  869.1 2.4 reshape.201
  877.9 2.8 copy.67
  883.0 3.1 fusion.79
  888.6 3.5 fusion.29
  (181 shorter events, 120.1 us)
Async XLA Ops:
  6.5 882.0 %copy-start = (bf16[1536,384]{1,0:T(8,128)(2,1)S(1)}, bf16[1536,384]{1,0:T(8,128)(2,1)}, u32[]{:S(2)}) copy-start(bf16[1536,384]{1,0:T(8,128)(2,1)} %param.19) | copy-start | bytes 3538948
  9.8 33.5 %all-to-all-start = ((s32[128,1,1]{2,1,0:T(1,128)}), s32[128,1,1]{2,1,0:T(1,128)S(1)}, u32[]{:S(2)}, u32[]{:S(2)}) async-start(s32[128,1,1]{2,1,0:T(1,128)} %copy.50), calls=%async_computation | async-start | bytes 131072 | tf_op jit(solution)/shard_map/all_to_all | solution.py:66
  30.1 0.8 copy-start.3
  33.1 20.9 %copy-start.2 = (bf16[512,768]{1,0:T(8,128)(2,1)}, bf16[512,768]{1,0:T(8,128)(2,1)S(1)}, u32[]{:S(2)}) copy-start(bf16[512,768]{1,0:T(8,128)(2,1)S(1)} %slice.35) | copy-start | bytes 2359300
  53.9 10.0 %copy-start.4 = (s32[128]{0:T(128)S(1)}, s32[128]{0:T(128)}, u32[]{:S(2)}) copy-start(s32[128]{0:T(128)} %param.13) | copy-start | bytes 1540
  53.9 554.8 %all-to-all-start.1 = ((bf16[128,1,64,768]{3,2,1,0:T(8,128)(2,1)}), bf16[128,1,64,768]{3,2,1,0:T(8,128)(2,1)}, u32[]{:S(2)}, u32[]{:S(2)}) async-start(bf16[128,1,64,768]{3,2,1,0:T(8,128)(2,1)} %bitcast.77), calls=%async_computation.1 | async-start | bytes 25165824 | tf_op jit(solution)/shard_map/all_to_all | solution.py:70
  61.5 50.5 %all-gather.2.cloned.1.call-start = ((), (), s32[]{:S(2)}) async-start(), calls=%async_computation.2 | async-start | bytes 3932160 | tf_op jit(solution)/shard_map/all_gather | solution.py:50
  631.8 1.9 copy-start.1
  666.6 1.9 copy-start.1
  701.4 1.9 copy-start.1
  736.2 1.9 copy-start.1
  770.9 1.9 copy-start.1
  805.7 1.9 copy-start.1
  840.5 1.9 copy-start.1
  875.3 1.9 copy-start.1
Sparse Core Ops, SparseCore 0:
  64.5 47.5 all-gather.1
where the time goes:
time: 903 us; the launch traced here: 900 us
  waiting for transfers between devices  554 us (61%)
  local copies, waits for them, and re-layouts  236 us (26%)
  matrix products  48.5 us (5%)
  starting transfers between devices  27 us (3%)
  other arithmetic  21.2 us (2%)
  between operations  13.5 us (1%)
    all_to_all x1, waiting for transfers between devices, body(): lax.all_to_all(kv_sent, 'gz', split_axis=0, concat_axis=0, tiled=True)  497 us
    gather x16, local copies, waits for them, and re-layouts, one_block(): gathered = jnp.concatenate([slab_kv[near_row], far_kv[slot_row]], axis=0)  61.5 us
    all_gather x1, waiting for transfers between devices, body(): slab_kv = lax.all_gather(kv_own, 'row', axis=0, tiled=True)  46.3 us
    slice x16, local copies, waits for them, and re-layouts, attend(): keys = key_values[:, :, :model_width].reshape(-1, H, head_size)  46.1 us
    dot_general x8, matrix products, attend(): jnp.einsum('hqk,khd->qhd', weights.astype(jnp.bfloat16), values, preferre...  25.1 us
    slice x8, local copies, waits for them, and re-layouts, attend(): values = key_values[:, :, model_width:].reshape(-1, H, head_size)  22.3 us
    while x24, local copies, waits for them, and re-layouts  21.4 us
    all_to_all x1, starting transfers between devices, body(): lax.all_to_all(request.reshape(slabs_n, per_owner), 'gz', split_axis=0, c...  19.2 us
  transfers between devices with their start and end apart: 3, of which 3 were waited for; matrix products, arithmetic and copies ran while one was open for 1% of the time, Pallas kernels for 0%

commit v1 on v0

--- a/solution.py
+++ b/solution.py
@@ -6,6 +6,28 @@
 H = 12
 NNEAR = 4
 NFAR = 16
+
+
+def laid_out(blocks, dim):
+    blocks = jnp.moveaxis(blocks, 0, dim)
+    lengths = blocks.shape
+    return blocks.reshape(*lengths[:dim], lengths[dim] * lengths[dim + 1], *lengths[dim + 2 :])
+
+
+def gather_around(x, axis, dim):
+    size = lax.axis_size(axis)
+    pairs = [(i, (i + 1) % size) for i in range(size)]
+    back = [(b, a) for a, b in pairs]
+    lower, upper = ([], [])
+    for step in range(size - 1):
+        if step % 2 == 0:
+            lower.append(lax.ppermute(lower[-1] if lower else x, axis, pairs))
+        else:
+            upper.append(lax.ppermute(upper[-1] if upper else x, axis, back))
+    blocks = jnp.stack([*lower[::-1], x, *upper])
+    shift = lax.axis_index(axis) - len(lower)
+    blocks = blocks[(jnp.arange(size) - shift) % size]
+    return laid_out(blocks, dim)
 
 
 def rms_norm(values, gain):
@@ -47,7 +69,7 @@
     projected = jnp.dot(normed, qkv_weight, preferred_element_type=jnp.float32).astype(jnp.bfloat16)
     queries = projected[:, :model_width].reshape(own_blocks, block_len, model_width)
     kv_own = projected[:, model_width:].reshape(own_blocks, block_len, 2 * model_width)
-    slab_kv = lax.all_gather(kv_own, "row", axis=0, tiled=True)
+    slab_kv = gather_around(kv_own, "row", 0)
     owner_slab = key_blocks // slab_blocks
     within = key_blocks % slab_blocks
     slab_table = jnp.arange(slabs_n, dtype=jnp.int32)

time: 903 us -> 842 us (0.932)
  matrix products: 48.5 us -> 29.6 us
  waiting for transfers between devices: 554 us -> 537 us
  local copies, waits for them, and re-layouts: 236 us -> 220 us
  between operations: 13.5 us -> 0.19 us
    all_gather x1 -> x0, waiting for transfers between devices: 46.3 us -> none  [body(): slab_kv = lax.all_gather(kv_own, 'row', axis=0, tiled=True)]
    ppermute x0 -> x3, waiting for transfers between devices: none -> 30 us  [the longest x2 30 us: gather_around(): lower.append(lax.ppermute(lower[-1] if lower else x, axis, pairs))]
    dot_general x8, matrix products: 25.1 us -> 5.77 us  [attend(): jnp.einsum('hqk,khd->qhd', weights.astype(jnp.bfloat16), values, preferre...]
    while x24 -> x120, local copies, waits for them, and re-layouts: 21.4 us -> 10 us
    select_n x16, other arithmetic: 10.9 us -> 0.19 us  [one_block(): gathered = jnp.concatenate([slab_kv[near_row], far_kv[slot_row]], axis=0)]
    ppermute x0 -> x3, starting transfers between devices: none -> 9.41 us  [the longest x2 6.96 us: gather_around(): lower.append(lax.ppermute(lower[-1] if lower else x, axis, pairs))]
  transfers between devices with their start and end apart: 3 -> 5, of which waited for: 3 -> 4; matrix products, arithmetic and copies ran while one was open for 1% -> 2% of each run, Pallas kernels for 0% -> 0%
where the time goes in v1:
time: 842 us; the launch traced here: 840 us
  waiting for transfers between devices  537 us (64%)
  local copies, waits for them, and re-layouts  220 us (26%)
  starting transfers between devices  36 us (4%)
  matrix products  29.6 us (4%)
  other arithmetic  15.6 us (2%)
    all_to_all x1, waiting for transfers between devices, body(): lax.all_to_all(kv_sent, 'gz', split_axis=0, concat_axis=0, tiled=True)  497 us
    gather x16, local copies, waits for them, and re-layouts, one_block(): gathered = jnp.concatenate([slab_kv[near_row], far_kv[slot_row]], axis=0)  61.4 us
    slice x16, local copies, waits for them, and re-layouts, attend(): keys = key_values[:, :, :model_width].reshape(-1, H, head_size)  46.2 us
    ppermute x2, waiting for transfers between devices, gather_around(): lower.append(lax.ppermute(lower[-1] if lower else x, axis, pairs))  30 us
    slice x8, local copies, waits for them, and re-layouts, attend(): values = key_values[:, :, model_width:].reshape(-1, H, head_size)  22.3 us
    all_to_all x1, starting transfers between devices, body(): lax.all_to_all(request.reshape(slabs_n, per_owner), 'gz', split_axis=0, c...  19.2 us
    reshape x8, local copies, waits for them, and re-layouts, attend(): values = key_values[:, :, model_width:].reshape(-1, H, head_size)  19 us
    reshape x8, local copies, waits for them, and re-layouts, attend(): keys = key_values[:, :, :model_width].reshape(-1, H, head_size)  18.6 us
  transfers between devices with their start and end apart: 5, of which 4 were waited for; matrix products, arithmetic and copies ran while one was open for 2% of the time, Pallas kernels for 0%

profile of v1, /device:TPU:34, one launch (start us, length us, event | category | flops | bytes accessed | tf_op | source)
XLA Modules:
  0.0 839.6 jit_solution(14190456981781282104)
XLA Ops:
  3.8 19.2 %all-to-all-start = ((s32[128,1,1]{2,1,0:T(1,128)}), s32[128,1,1]{2,1,0:T(1,128)S(1)}, u32[]{:S(2)}, u32[]{:S(2)}) async-start(s32[128,1,1]{2,1,0:T(1,128)} %copy.48), calls=%async_computation | async-start | bytes 131072 | tf_op jit(solution)/shard_map/all_to_all | solution.py:88
  27.1 10.2 %all-to-all-done = s32[128,1,1]{2,1,0:T(1,128)S(1)} async-done(((s32[128,1,1]{2,1,0:T(1,128)}), s32[128,1,1]{2,1,0:T(1,128)S(1)}, u32[]{:S(2)}, u32[]{:S(2)}) %all-to-all-start) | async-done | bytes 544 | tf_op jit(solution)/shard_map/all_to_all | solution.py:88
  37.3 2.3 reduce
  39.7 8.3 gather_fusion.3
  48.0 7.5 all-to-all-start.1
  55.4 3.4 collective-permute-start
  58.9 2.4 collective-permute-start.2
  62.2 14.8 %collective-permute-done = bf16[8,64,768]{2,1,0:T(8,128)(2,1)} collective-permute-done((bf16[8,64,768]{2,1,0:T(8,128)(2,1)S(1)}, bf16[8,64,768]{2,1,0:T(8,128)(2,1)}, u32[]{:S(2)}, u32[]{:S(2)}) %collective-permute-start) | collective-permute-done | bytes 786464 | tf_op jit(solution)/shard_map/ppermute | solution.py:24
  77.0 3.6 collective-permute-start.1
  82.8 15.1 %collective-permute-done.1 = bf16[8,64,768]{2,1,0:T(8,128)(2,1)S(1)} collective-permute-done((bf16[8,64,768]{2,1,0:T(8,128)(2,1)}, bf16[8,64,768]{2,1,0:T(8,128)(2,1)S(1)}, u32[]{:S(2)}, u32[]{:S(2)}) %collective-permute-start.1) | collective-permute-done | bytes 786464 | tf_op jit(solution)/shard_map/ppermute | solution.py:24
  97.9 3.1 pad_maximum_fusion
  101.0 4.4 gather_fusion.2
  105.4 497.3 %all-to-all-done.1 = bf16[128,1,64,768]{3,2,1,0:T(8,128)(2,1)} async-done(((bf16[128,1,64,768]{3,2,1,0:T(8,128)(2,1)}), bf16[128,1,64,768]{3,2,1,0:T(8,128)(2,1)}, u32[]{:S(2)}, u32[]{:S(2)}) %all-to-all-start.1) | async-done | bytes 12582944 | tf_op jit(solution)/shard_map/all_to_all | solution.py:92
  602.6 230.8 %while.10 = (s32[]{:T(128)}, bf16[8,64,384]{2,1,0:T(8,128)(2,1)}, s32[8,4]{1,0:T(8,128)S(1)}, bf16[32,64,768]{2,1,0:T(8,128)(2,1)}, s32[8,16]{1,0:T(8,128)S(1)},...) while((s32[]{:T(128)}, bf16[8,64,384]{2,1,0:T(8,128)(2,1)}, ...), condition=%wide.region_8.9_spmd, body=%wide.region_5.8_spmd.sunk | while | flops 132760128 | bytes 41024440 | solution.py:102
  603.6 2.5 gather_fusion
  606.9 5.2 gather_fusion.1
  613.4 3.0 fusion.78
  616.4 2.8 copy.64
  619.2 2.4 reshape.261
  621.6 2.8 copy.66
  624.4 2.3 reshape.262
  632.5 2.5 gather_fusion
  635.8 5.2 gather_fusion.1
  642.3 3.0 fusion.78
  645.3 2.8 copy.64
  648.1 2.4 reshape.261
  650.5 2.8 copy.66
  661.4 2.5 gather_fusion
  664.6 5.2 gather_fusion.1
  671.2 3.0 fusion.78
  674.1 2.8 copy.64
  676.9 2.4 reshape.261
  679.3 2.8 copy.66
  690.2 2.5 gather_fusion
  693.5 5.2 gather_fusion.1
  700.0 3.0 fusion.78
  703.0 2.8 copy.64
  705.8 2.4 reshape.261
  708.2 2.8 copy.66
  719.1 2.5 gather_fusion
  722.3 5.2 gather_fusion.1
  728.9 3.0 fusion.78
  731.9 2.8 copy.64
  734.7 2.4 reshape.261
  737.0 2.8 copy.66
  747.9 2.5 gather_fusion
  751.2 5.2 gather_fusion.1
  757.7 3.0 fusion.78
  760.7 2.8 copy.64
  763.5 2.4 reshape.261
  765.9 2.8 copy.66
  776.8 2.5 gather_fusion
  780.1 5.2 gather_fusion.1
  786.6 3.0 fusion.78
  789.6 2.8 copy.64
  792.4 2.4 reshape.261
  794.7 2.8 copy.66
  805.6 2.5 gather_fusion
  808.9 5.2 gather_fusion.1
  815.4 3.0 fusion.78
  818.4 2.8 copy.64
  821.2 2.4 reshape.261
  823.6 2.8 copy.66
  835.1 3.5 fusion.29
  (284 shorter events, 92.0 us)
Async XLA Ops:
  0.0 835.1 %copy-start = (bf16[1536,384]{1,0:T(8,128)(2,1)S(1)}, bf16[1536,384]{1,0:T(8,128)(2,1)}, u32[]{:S(2)}) copy-start(bf16[1536,384]{1,0:T(8,128)(2,1)} %param.19) | copy-start | bytes 3538948
  1.6 0.9 copy-start.5
  3.8 33.5 %all-to-all-start = ((s32[128,1,1]{2,1,0:T(1,128)}), s32[128,1,1]{2,1,0:T(1,128)S(1)}, u32[]{:S(2)}, u32[]{:S(2)}) async-start(s32[128,1,1]{2,1,0:T(1,128)} %copy.48), calls=%async_computation | async-start | bytes 131072 | tf_op jit(solution)/shard_map/all_to_all | solution.py:88
  48.0 554.7 %all-to-all-start.1 = ((bf16[128,1,64,768]{3,2,1,0:T(8,128)(2,1)}), bf16[128,1,64,768]{3,2,1,0:T(8,128)(2,1)}, u32[]{:S(2)}, u32[]{:S(2)}) async-start(bf16[128,1,64,768]{3,2,1,0:T(8,128)(2,1)} %bitcast.84), calls=%async_computation.1 | async-start | bytes 25165824 | tf_op jit(solution)/shard_map/all_to_all | solution.py:92
  55.4 21.6 %collective-permute-start = (bf16[8,64,768]{2,1,0:T(8,128)(2,1)S(1)}, bf16[8,64,768]{2,1,0:T(8,128)(2,1)}, u32[]{:S(2)}, u32[]{:S(2)}) collective-permute-start(bf16[8,64,768]{2,1,0:T(8,128)(2,1)S(1)} %bitcast.81), channel_id=1, source_target_pairs={{0,1},{1,2},{2,3},{3,0},{4,5},{5,6},{6,7},{7,4},{8,9},{9,10},{10,1... | collective-permute-start | bytes 2359304 | tf_op jit(solution)/shard_map/ppermute | solution.py:24
  58.9 23.9 %collective-permute-start.2 = (bf16[8,64,768]{2,1,0:T(8,128)(2,1)S(1)}, bf16[8,64,768]{2,1,0:T(8,128)(2,1)}, u32[]{:S(2)}, u32[]{:S(2)}) collective-permute-start(bf16[8,64,768]{2,1,0:T(8,128)(2,1)S(1)} %bitcast.82), channel_id=1, source_target_pairs={{1,0},{2,1},{3,2},{0,3},{5,4},{6,5},{7,6},{4,7},{9,8},{10,9},{11,1... | collective-permute-start | bytes 2359304 | tf_op jit(solution)/shard_map/ppermute | solution.py:26
  77.0 20.9 %collective-permute-start.1 = (bf16[8,64,768]{2,1,0:T(8,128)(2,1)}, bf16[8,64,768]{2,1,0:T(8,128)(2,1)S(1)}, u32[]{:S(2)}, u32[]{:S(2)}) collective-permute-start(bf16[8,64,768]{2,1,0:T(8,128)(2,1)} %collective-permute-done), channel_id=1, source_target_pairs={{0,1},{1,2},{2,3},{3,0},{4,5},{5,6},{6,7},{7,4},{8,9},{9,10},{10,1... | collective-permute-start | bytes 2359304 | tf_op jit(solution)/shard_map/ppermute | solution.py:24
  602.6 232.5 %copy-start.10 = (f32[384]{0:T(512)S(1)}, f32[384]{0:T(512)}, u32[]{:S(2)}) copy-start(f32[384]{0:T(512)} %param.17) | copy-start | bytes 4612
  602.6 10.8 %copy-start.3 = (bf16[8,64,384]{2,1,0:T(8,128)(2,1)}, bf16[8,64,384]{2,1,0:T(8,128)(2,1)S(1)}, u32[]{:S(2)}) copy-start(bf16[8,64,384]{2,1,0:T(8,128)(2,1)S(1)} %get-tuple-element.200) | copy-start | bytes 1179652 | tf_op jit(solution)/shard_map/while
  602.6 10.8 %copy-start.6 = (s32[8,4]{1,0:T(8,128)}, s32[8,4]{1,0:T(8,128)S(1)}, u32[]{:S(2)}) copy-start(s32[8,4]{1,0:T(8,128)S(1)} %get-tuple-element.195) | copy-start | bytes 388 | tf_op jit(solution)/shard_map/while
  602.6 10.8 %copy-start.8 = (pred[8,20]{1,0:T(8,128)(4,1)}, pred[8,20]{1,0:T(8,128)(4,1)S(1)}, u32[]{:S(2)}) copy-start(pred[8,20]{1,0:T(8,128)(4,1)S(1)} %get-tuple-element.199) | copy-start | bytes 484 | tf_op jit(solution)/shard_map/while
  628.8 1.2 copy-start.1
  629.6 1.9 copy-start.4
  629.6 1.9 copy-start.7
  629.6 1.9 copy-start.9
  631.5 10.8 %copy-start.3 = (bf16[8,64,384]{2,1,0:T(8,128)(2,1)}, bf16[8,64,384]{2,1,0:T(8,128)(2,1)S(1)}, u32[]{:S(2)}) copy-start(bf16[8,64,384]{2,1,0:T(8,128)(2,1)S(1)} %get-tuple-element.200) | copy-start | bytes 1179652 | tf_op jit(solution)/shard_map/while
  631.5 10.8 %copy-start.6 = (s32[8,4]{1,0:T(8,128)}, s32[8,4]{1,0:T(8,128)S(1)}, u32[]{:S(2)}) copy-start(s32[8,4]{1,0:T(8,128)S(1)} %get-tuple-element.195) | copy-start | bytes 388 | tf_op jit(solution)/shard_map/while
  631.5 10.8 %copy-start.8 = (pred[8,20]{1,0:T(8,128)(4,1)}, pred[8,20]{1,0:T(8,128)(4,1)S(1)}, u32[]{:S(2)}) copy-start(pred[8,20]{1,0:T(8,128)(4,1)S(1)} %get-tuple-element.199) | copy-start | bytes 484 | tf_op jit(solution)/shard_map/while
  657.7 1.2 copy-start.1
  658.4 1.9 copy-start.4
  658.4 1.9 copy-start.7
  658.4 1.9 copy-start.9
  660.3 10.8 %copy-start.3 = (bf16[8,64,384]{2,1,0:T(8,128)(2,1)}, bf16[8,64,384]{2,1,0:T(8,128)(2,1)S(1)}, u32[]{:S(2)}) copy-start(bf16[8,64,384]{2,1,0:T(8,128)(2,1)S(1)} %get-tuple-element.200) | copy-start | bytes 1179652 | tf_op jit(solution)/shard_map/while
  660.3 10.8 %copy-start.6 = (s32[8,4]{1,0:T(8,128)}, s32[8,4]{1,0:T(8,128)S(1)}, u32[]{:S(2)}) copy-start(s32[8,4]{1,0:T(8,128)S(1)} %get-tuple-element.195) | copy-start | bytes 388 | tf_op jit(solution)/shard_map/while
  660.4 10.8 %copy-start.8 = (pred[8,20]{1,0:T(8,128)(4,1)}, pred[8,20]{1,0:T(8,128)(4,1)S(1)}, u32[]{:S(2)}) copy-start(pred[8,20]{1,0:T(8,128)(4,1)S(1)} %get-tuple-element.199) | copy-start | bytes 484 | tf_op jit(solution)/shard_map/while
  686.5 1.2 copy-start.1
  687.3 1.9 copy-start.4
  687.3 1.9 copy-start.7
  687.3 1.9 copy-start.9
  689.2 10.8 %copy-start.3 = (bf16[8,64,384]{2,1,0:T(8,128)(2,1)}, bf16[8,64,384]{2,1,0:T(8,128)(2,1)S(1)}, u32[]{:S(2)}) copy-start(bf16[8,64,384]{2,1,0:T(8,128)(2,1)S(1)} %get-tuple-element.200) | copy-start | bytes 1179652 | tf_op jit(solution)/shard_map/while
  689.2 10.8 %copy-start.6 = (s32[8,4]{1,0:T(8,128)}, s32[8,4]{1,0:T(8,128)S(1)}, u32[]{:S(2)}) copy-start(s32[8,4]{1,0:T(8,128)S(1)} %get-tuple-element.195) | copy-start | bytes 388 | tf_op jit(solution)/shard_map/while
  689.2 10.8 %copy-start.8 = (pred[8,20]{1,0:T(8,128)(4,1)}, pred[8,20]{1,0:T(8,128)(4,1)S(1)}, u32[]{:S(2)}) copy-start(pred[8,20]{1,0:T(8,128)(4,1)S(1)} %get-tuple-element.199) | copy-start | bytes 484 | tf_op jit(solution)/shard_map/while
  715.4 1.2 copy-start.1
  716.1 1.9 copy-start.4
  716.1 1.9 copy-start.7
  716.1 1.9 copy-start.9
  718.1 10.8 %copy-start.3 = (bf16[8,64,384]{2,1,0:T(8,128)(2,1)}, bf16[8,64,384]{2,1,0:T(8,128)(2,1)S(1)}, u32[]{:S(2)}) copy-start(bf16[8,64,384]{2,1,0:T(8,128)(2,1)S(1)} %get-tuple-element.200) | copy-start | bytes 1179652 | tf_op jit(solution)/shard_map/while
  718.1 10.8 %copy-start.6 = (s32[8,4]{1,0:T(8,128)}, s32[8,4]{1,0:T(8,128)S(1)}, u32[]{:S(2)}) copy-start(s32[8,4]{1,0:T(8,128)S(1)} %get-tuple-element.195) | copy-start | bytes 388 | tf_op jit(solution)/shard_map/while
  718.1 10.8 %copy-start.8 = (pred[8,20]{1,0:T(8,128)(4,1)}, pred[8,20]{1,0:T(8,128)(4,1)S(1)}, u32[]{:S(2)}) copy-start(pred[8,20]{1,0:T(8,128)(4,1)S(1)} %get-tuple-element.199) | copy-start | bytes 484 | tf_op jit(solution)/shard_map/while
  744.2 1.2 copy-start.1
  745.0 1.9 copy-start.4
  745.0 1.9 copy-start.7
  745.0 1.9 copy-start.9
  746.9 10.8 %copy-start.3 = (bf16[8,64,384]{2,1,0:T(8,128)(2,1)}, bf16[8,64,384]{2,1,0:T(8,128)(2,1)S(1)}, u32[]{:S(2)}) copy-start(bf16[8,64,384]{2,1,0:T(8,128)(2,1)S(1)} %get-tuple-element.200) | copy-start | bytes 1179652 | tf_op jit(solution)/shard_map/while
  746.9 10.8 %copy-start.6 = (s32[8,4]{1,0:T(8,128)}, s32[8,4]{1,0:T(8,128)S(1)}, u32[]{:S(2)}) copy-start(s32[8,4]{1,0:T(8,128)S(1)} %get-tuple-element.195) | copy-start | bytes 388 | tf_op jit(solution)/shard_map/while
  746.9 10.8 %copy-start.8 = (pred[8,20]{1,0:T(8,128)(4,1)}, pred[8,20]{1,0:T(8,128)(4,1)S(1)}, u32[]{:S(2)}) copy-start(pred[8,20]{1,0:T(8,128)(4,1)S(1)} %get-tuple-element.199) | copy-start | bytes 484 | tf_op jit(solution)/shard_map/while
  773.1 1.2 copy-start.1
  773.8 1.9 copy-start.4
  773.9 1.9 copy-start.7
  773.9 1.9 copy-start.9
  775.8 10.8 %copy-start.3 = (bf16[8,64,384]{2,1,0:T(8,128)(2,1)}, bf16[8,64,384]{2,1,0:T(8,128)(2,1)S(1)}, u32[]{:S(2)}) copy-start(bf16[8,64,384]{2,1,0:T(8,128)(2,1)S(1)} %get-tuple-element.200) | copy-start | bytes 1179652 | tf_op jit(solution)/shard_map/while
  775.8 10.8 %copy-start.6 = (s32[8,4]{1,0:T(8,128)}, s32[8,4]{1,0:T(8,128)S(1)}, u32[]{:S(2)}) copy-start(s32[8,4]{1,0:T(8,128)S(1)} %get-tuple-element.195) | copy-start | bytes 388 | tf_op jit(solution)/shard_map/while
  775.8 10.8 %copy-start.8 = (pred[8,20]{1,0:T(8,128)(4,1)}, pred[8,20]{1,0:T(8,128)(4,1)S(1)}, u32[]{:S(2)}) copy-start(pred[8,20]{1,0:T(8,128)(4,1)S(1)} %get-tuple-element.199) | copy-start | bytes 484 | tf_op jit(solution)/shard_map/while
  801.9 1.2 copy-start.1
  802.7 1.9 copy-start.4
  802.7 1.9 copy-start.7
  802.7 1.9 copy-start.9
  804.6 10.8 %copy-start.3 = (bf16[8,64,384]{2,1,0:T(8,128)(2,1)}, bf16[8,64,384]{2,1,0:T(8,128)(2,1)S(1)}, u32[]{:S(2)}) copy-start(bf16[8,64,384]{2,1,0:T(8,128)(2,1)S(1)} %get-tuple-element.200) | copy-start | bytes 1179652 | tf_op jit(solution)/shard_map/while
  804.6 10.8 %copy-start.6 = (s32[8,4]{1,0:T(8,128)}, s32[8,4]{1,0:T(8,128)S(1)}, u32[]{:S(2)}) copy-start(s32[8,4]{1,0:T(8,128)S(1)} %get-tuple-element.195) | copy-start | bytes 388 | tf_op jit(solution)/shard_map/while
  804.6 10.8 %copy-start.8 = (pred[8,20]{1,0:T(8,128)(4,1)}, pred[8,20]{1,0:T(8,128)(4,1)S(1)}, u32[]{:S(2)}) copy-start(pred[8,20]{1,0:T(8,128)(4,1)S(1)} %get-tuple-element.199) | copy-start | bytes 484 | tf_op jit(solution)/shard_map/while
  830.8 1.2 copy-start.1
  831.6 1.9 copy-start.4
  831.6 1.9 copy-start.7
  831.6 1.9 copy-start.9
  (1 other events, 0.8 us)
